TPU v7x, 32 devices: a whole 2x2x4 slice. The times are simulated.
32 devices in a mesh: gx: 8 (over z, core), gy: 4 (over y, x).
Axes of the slice: x: 2, y: 2, z: 4, core: 2. Of those that a mesh axis runs over, the one named last changes fastest.
Arguments:
- init_re: float32 [1, 256, 4096], P(None, 'gx', 'gy'), may hold values from -6 to 6
- init_im: float32 [1, 256, 4096], P(None, 'gx', 'gy'), may hold values from -6 to 6
- onsite: float32 [256, 4096], P('gx', 'gy'), may hold values from -0.9 to 0.9
- bond_x: int32 [256, 4096], P('gx', 'gy'), may hold values from 0 to 15
- bond_y: int32 [256, 4096], P('gx', 'gy'), may hold values from 0 to 15
- hop_table: float32 [16], replicated, may hold values from 1.4 to 1.6
- centre: int32 [1, 2], replicated, may hold values from 0 to 255
- duration: float32 [1], replicated, may hold values from 0.55 to 0.6
Outputs:
- out_re: float32 [1, 256, 4096], P(None, 'gx', 'gy')
- out_im: float32 [1, 256, 4096], P(None, 'gx', 'gy')
- term_norms: float32 [2, 8, 1], replicated
All inputs are finite; a program needn't handle non-finite values.
Results may differ from a plain program's by a relative error of at most 0.0003.
Values sent between devices are 32-bit elements; how exact they have to be, the bound alone decides.
A program may use at most 64 MiB of HBM per device.

v0:
```python
import math

import jax
import jax.numpy as jnp
from jax import lax
from jax.sharding import PartitionSpec as P

TERMS = 8
STEPS = 2


SPECTRAL = 7.5
epsilon = 1e-06


def padded(block, sides, width):
    for axis, dim in sides:
        count = lax.axis_size(axis)
        forward = [(i, i + 1) for i in range(count - 1)]
        forward.append((count - 1, 0))
        backward = [(target, source) for source, target in forward]
        low = lax.ppermute(
            lax.slice_in_dim(block, block.shape[dim] - width, None, axis=dim), axis, forward
        )
        high = lax.ppermute(lax.slice_in_dim(block, 0, width, axis=dim), axis, backward)
        block = jnp.concatenate([low, block, high], axis=dim)
    return block


def bessel_weights(duration):
    argument = duration[0] * SPECTRAL
    halved = argument * 0.5
    weights = []
    for degree in range(TERMS):
        series = halved**degree / math.factorial(degree)
        summed = series
        for counter in range(1, 24):
            series = series * -(halved * halved) / (counter * (counter + degree))
            summed = summed + series
        weights.append(summed if degree == 0 else 2.0 * summed)
    return weights


def rotated(degree, real_part, imag_part):
    quarter = degree % 4
    if quarter == 0:
        return (real_part, imag_part)
    if quarter == 1:
        return (imag_part, -real_part)
    if quarter == 2:
        return (-real_part, -imag_part)
    return (-imag_part, real_part)


def falloff(positions, centres, extent):
    distance = jnp.mod(positions[None, :] - centres[:, None], extent)
    distance = jnp.minimum(distance, extent - distance).astype(jnp.float32)
    return distance * distance * (4.5 / (extent * extent))


def shrink(tensor, margin):
    if margin == 0:
        return tensor
    return tensor[..., margin : tensor.shape[-2] - margin, margin : tensor.shape[-1] - margin]


def apply_wide(grid_field, coeffs):
    potential = coeffs[0]
    hop_rows = coeffs[1]
    hop_cols = coeffs[2]
    result = potential[1:-1, 1:-1] * grid_field[..., 1:-1, 1:-1]
    result = result - hop_rows[1:-1, 1:-1] * grid_field[..., 2:, 1:-1]
    result = result - hop_rows[:-2, 1:-1] * grid_field[..., :-2, 1:-1]
    result = result - hop_cols[1:-1, 1:-1] * grid_field[..., 1:-1, 2:]
    result = result - hop_cols[1:-1, :-2] * grid_field[..., 1:-1, :-2]
    return result * (1.0 / SPECTRAL)


def per_device(init_re, init_im, onsite, bond_x, bond_y, hop_table, centre, duration):
    packets, rows_local, cols_local = init_re.shape
    rows_total = rows_local * lax.axis_size("gx")
    cols_total = cols_local * lax.axis_size("gy")
    cell_count = rows_total * cols_total
    classes = hop_table.shape[0]
    selector = jnp.arange(classes, dtype=jnp.int32)[:, None, None]
    table_column = hop_table[:, None, None]
    hop_down = jnp.sum(jnp.where(bond_x[None] == selector, table_column, 0.0), axis=0)
    hop_right = jnp.sum(jnp.where(bond_y[None] == selector, table_column, 0.0), axis=0)
    weights = bessel_weights(duration)
    row_index = lax.axis_index("gx") * rows_local + lax.iota(jnp.int32, rows_local)
    col_index = lax.axis_index("gy") * cols_local + lax.iota(jnp.int32, cols_local)
    row_fall = falloff(row_index, centre[:, 0], rows_total)
    col_fall = falloff(col_index, centre[:, 1], cols_total)
    envelope = jnp.exp(-(row_fall[:, :, None] + col_fall[:, None, :]))
    packet_state = jnp.stack([init_re * envelope, init_im * envelope])
    reach = TERMS - 1
    coeffs = padded(jnp.stack([onsite, hop_down, hop_right]), (("gx", 1), ("gy", 2)), reach)
    norm_rows = []
    for repeat in range(STEPS):
        current = padded(packet_state, (("gx", 2), ("gy", 3)), reach)
        margin = reach
        previous = current
        previous_margin = reach
        chebyshev = [packet_state]
        for chebyshev_degree in range(1, TERMS):
            applied = apply_wide(current, shrink(coeffs, reach - margin))
            if chebyshev_degree == 1:
                following = applied
            else:
                following = 2.0 * applied - shrink(previous, previous_margin - margin + 1)
            previous, previous_margin = (current, margin)
            current = following
            margin = margin - 1
            chebyshev.append(shrink(following, margin))
        accumulate = weights[0] * packet_state
        for degree in range(1, TERMS):
            real_rot, imag_rot = rotated(degree, chebyshev[degree][0], chebyshev[degree][1])
            accumulate = accumulate + weights[degree] * jnp.stack([real_rot, imag_rot])
        term_local = jnp.stack([jnp.sum(vector * vector, axis=(0, 2, 3)) for vector in chebyshev])
        state_local = jnp.sum(accumulate * accumulate, axis=(0, 2, 3))
        term_total, state_total = lax.psum((term_local, state_local), ("gx", "gy"))
        norm_rows.append(term_total / cell_count)
        rescale = lax.rsqrt(state_total / cell_count + epsilon)
        packet_state = accumulate * rescale[None, :, None, None]
    return (packet_state[0], packet_state[1], jnp.stack(norm_rows))


def solution(mesh):
    return jax.shard_map(
        per_device,
        mesh=mesh,
        in_specs=(
            P(None, "gx", "gy"),
            P(None, "gx", "gy"),
            P("gx", "gy"),
            P("gx", "gy"),
            P("gx", "gy"),
            P(),
            P(),
            P(),
        ),
        out_specs=(P(None, "gx", "gy"), P(None, "gx", "gy"), P()),
        check_vma=False,
    )
```

profile of v0, /device:TPU:0, one launch (start us, length us, event | category | flops | bytes accessed | tf_op | source)
XLA Modules:
  0.0 153.5 jit_solution(4384548073286884623)
XLA Ops:
  0.7 1.3 fusion.128
  2.0 0.7 fusion.100
  2.6 0.7 fusion.97
  3.3 1.1 multiply_bitcast_fusion
  4.4 0.5 collective-permute-start.4
  5.0 4.1 %collective-permute-start.5 = (f32[2,1,7,1024]{3,2,1,0:T(8,128)S(1)}, f32[2,1,7,1024]{3,2,1,0:T(8,128)S(1)}, u32[]{:S(2)}, u32[]{:S(2)}) collective-permute-start(f32[2,1,7,1024]{3,2,1,0:T(8,128)S(1)} %get-tuple-element.80), channel_id=1, source_target_pairs={{4,0},{8,4},{12,8},{16,12},{20,16},{24,20},{28,24},{0,28},{5,1},{9... | collective-permute-start | bytes 172040 | tf_op jit(solution)/shard_map/ppermute | solution.py:25
  9.7 3.5 %collective-permute-start.1 = (f32[3,7,1024]{2,1,0:T(8,128)S(1)}, f32[3,7,1024]{2,1,0:T(8,128)S(1)}, u32[]{:S(2)}, u32[]{:S(2)}) collective-permute-start(f32[3,7,1024]{2,1,0:T(8,128)S(1)} %get-tuple-element.52), channel_id=1, source_target_pairs={{4,0},{8,4},{12,8},{16,12},{20,16},{24,20},{28,24},{0,28},{5,1},{9... | collective-permute-start | bytes 258056 | tf_op jit(solution)/shard_map/ppermute | solution.py:25
  14.5 0.7 multiply_reduce_fusion.9
  16.0 3.4 %collective-permute-start.3 = (f32[3,46,7]{2,1,0:T(8,128)S(1)}, f32[3,46,7]{2,1,0:T(8,128)S(1)}, u32[]{:S(2)}, u32[]{:S(2)}) collective-permute-start(f32[3,46,7]{2,1,0:T(8,128)S(1)} %get-tuple-element.39), channel_id=1, source_target_pairs={{1,0},{2,1},{3,2},{0,3},{5,4},{6,5},{7,6},{4,7},{9,8},{10,9},{11,1... | collective-permute-start | bytes 11600 | tf_op jit(solution)/shard_map/ppermute | solution.py:25
  19.4 2.9 %collective-permute-start.7 = (f32[2,1,46,7]{3,2,1,0:T(8,128)S(1)}, f32[2,1,46,7]{3,2,1,0:T(8,128)S(1)}, u32[]{:S(2)}, u32[]{:S(2)}) collective-permute-start(f32[2,1,46,7]{3,2,1,0:T(8,128)S(1)} %get-tuple-element.53), channel_id=1, source_target_pairs={{1,0},{2,1},{3,2},{0,3},{5,4},{6,5},{7,6},{4,7},{9,8},{10,9},{11,1... | collective-permute-start | bytes 7736 | tf_op jit(solution)/shard_map/ppermute | solution.py:25
  22.4 1.8 %collective-permute-done.7 = f32[2,1,46,7]{3,2,1,0:T(8,128)S(1)} collective-permute-done((f32[2,1,46,7]{3,2,1,0:T(8,128)S(1)}, f32[2,1,46,7]{3,2,1,0:T(8,128)S(1)}, u32[]{:S(2)}, u32[]{:S(2)}) %collective-permute-start.7) | collective-permute-done | bytes 2608 | tf_op jit(solution)/shard_map/ppermute | solution.py:25
  24.2 3.2 %collective-permute-done.6 = f32[2,1,46,7]{3,2,1,0:T(8,128)S(1)} collective-permute-done((f32[2,1,46,7]{3,2,1,0:T(8,128)S(1)}, f32[2,1,46,7]{3,2,1,0:T(8,128)S(1)}, u32[]{:S(2)}, u32[]{:S(2)}) %collective-permute-start.6) | collective-permute-done | bytes 2608 | tf_op jit(solution)/shard_map/ppermute | solution.py:22
  29.7 0.5 fusion.16
  30.3 0.8 fusion.65
  31.6 0.7 slice_subtract_fusion.1
  32.3 0.8 fusion.64
  34.5 0.6 slice_subtract_fusion.9
  35.7 0.6 slice_subtract_fusion.8
  36.6 0.6 slice_subtract_fusion.7
  37.6 0.6 slice_subtract_fusion.6
  38.8 1.1 multiply_reduce_fusion.5
  39.9 0.9 multiply_reduce_fusion.11
  40.8 37.0 %psum.28 = f32[1]{0:T(128)} all-reduce(f32[1]{0:T(128)} %bitcast.29), channel_id=1, replica_groups=mesh['gx'=8,'gy'=4] {'gx','gy'}, use_global_device_ids=true, to_apply=%region_3.4 | all-reduce | flops 1 | bytes 8 | tf_op jit(solution)/shard_map/psum | solution.py:121
  78.5 0.7 multiply_reduce_fusion.4
  79.3 3.5 %collective-permute-start.9 = (f32[2,1,7,1024]{3,2,1,0:T(8,128)S(1)}, f32[2,1,7,1024]{3,2,1,0:T(8,128)S(1)}, u32[]{:S(2)}, u32[]{:S(2)}) collective-permute-start(f32[2,1,7,1024]{3,2,1,0:T(8,128)S(1)} %get-tuple-element.76), channel_id=1, source_target_pairs={{4,0},{8,4},{12,8},{16,12},{20,16},{24,20},{28,24},{0,28},{5,1},{9... | collective-permute-start | bytes 172040 | tf_op jit(solution)/shard_map/ppermute | solution.py:25
  82.8 0.7 fusion.63
  83.5 1.2 collective-permute-done.8
  84.9 2.5 %collective-permute-start.11 = (f32[2,1,46,7]{3,2,1,0:T(8,128)S(1)}, f32[2,1,46,7]{3,2,1,0:T(8,128)S(1)}, u32[]{:S(2)}, u32[]{:S(2)}) collective-permute-start(f32[2,1,46,7]{3,2,1,0:T(8,128)S(1)} %get-tuple-element.49), channel_id=1, source_target_pairs={{1,0},{2,1},{3,2},{0,3},{5,4},{6,5},{7,6},{4,7},{9,8},{10,9},{11,1... | collective-permute-start | bytes 7736 | tf_op jit(solution)/shard_map/ppermute | solution.py:25
  87.4 0.8 multiply_reduce_fusion.8
  88.1 5.1 %stack.171 = f32[8,1]{0,1:T(1,128)S(1)} concatenate(f32[1,1]{0,1:T(1,128)} %bitcast.35, f32[1,1]{0,1:T(1,128)} %bitcast.36, f32[1,1]{0,1:T(1,128)} %bitcast.37, f32[1,1]{0,1:T(1,128)} %bitcast.38, f32[1,1]{0,1:T(1,128)} %bitcast.39, f32[1,1]{0,1:T(1,128)} %bitcast.40, f32[1,1]{0,1:T(1,128)} %bitcast.41, f32[1,1]{0,1:T(1,128)} %bitcast.42), dimensions={0} | concatenate | bytes 64 | tf_op jit(solution)/shard_map/stack | solution.py:119
  93.3 0.6 copy-done.53
  93.9 1.1 concatenate.135
  95.5 0.8 fusion.62
  96.4 0.7 slice_subtract_fusion
  97.0 0.8 fusion.61
  97.9 0.6 slice_subtract_fusion.5
  98.4 0.8 fusion.60
  99.3 0.6 slice_subtract_fusion.4
  99.8 0.8 multiply_reduce_fusion.3
  100.7 0.6 slice_subtract_fusion.3
  101.6 0.6 copy-done.3
  102.5 0.6 slice_subtract_fusion.2
  103.6 1.0 multiply_reduce_fusion
  105.1 5.2 %stack.181 = f32[8,1]{0,1:T(1,128)S(1)} concatenate(f32[1,1]{0,1:T(1,128)} %bitcast.44, f32[1,1]{0,1:T(1,128)} %bitcast.45, f32[1,1]{0,1:T(1,128)} %bitcast.46, f32[1,1]{0,1:T(1,128)} %bitcast.47, f32[1,1]{0,1:T(1,128)} %bitcast.48, f32[1,1]{0,1:T(1,128)} %bitcast.49, f32[1,1]{0,1:T(1,128)} %bitcast.50, f32[1,1]{0,1:T(1,128)} %bitcast.51), dimensions={0} | concatenate | bytes 64 | tf_op jit(solution)/shard_map/stack | solution.py:119
  110.3 0.8 multiply_reduce_fusion.10
  111.1 40.4 %all-reduce = (f32[1]{0:T(128)}, f32[8,1]{0,1:T(1,128)S(1)}, f32[8,1]{0,1:T(1,128)S(1)}) all-reduce(f32[1]{0:T(128)} %bitcast.31, f32[8,1]{0,1:T(1,128)S(1)} %stack.181, f32[8,1]{0,1:T(1,128)S(1)} %stack.171), channel_id=1, replica_groups=mesh['gx'=8,'gy'=4] {'gx','gy'}, use_global_device_ids=true, to_apply=%region_5.6 | all-reduce | flops 17 | bytes 136 | tf_op jit(solution)/shard_map/psum | solution.py:121
  152.2 0.7 slice_bitcast_fusion.21
  153.0 0.6 pad_maximum_fusion.7
  (171 shorter events, 9.8 us)
Async XLA Ops:
  0.6 8.4 %copy-start.54 = (f32[16]{0:T(128)S(1)}, f32[16]{0:T(128)}, u32[]{:S(2)}) copy-start(f32[16]{0:T(128)} %param.13) | copy-start | bytes 196
  0.6 8.4 %copy-start.52 = (s32[32,1024]{1,0:T(8,128)S(1)}, s32[32,1024]{1,0:T(8,128)}, u32[]{:S(2)}) copy-start(s32[32,1024]{1,0:T(8,128)} %param.12) | copy-start | bytes 393220
  0.7 8.4 %copy-start.51 = (s32[32,1024]{1,0:T(8,128)S(1)}, s32[32,1024]{1,0:T(8,128)}, u32[]{:S(2)}) copy-start(s32[32,1024]{1,0:T(8,128)} %param.11) | copy-start | bytes 393220
  3.3 6.3 %copy-start.50 = (f32[32,1024]{1,0:T(8,128)S(1)}, f32[32,1024]{1,0:T(8,128)}, u32[]{:S(2)}) copy-start(f32[32,1024]{1,0:T(8,128)} %param.10) | copy-start | bytes 393220
  4.4 10.8 %collective-permute-start.4 = (f32[2,1,7,1024]{3,2,1,0:T(8,128)S(1)}, f32[2,1,7,1024]{3,2,1,0:T(8,128)S(1)}, u32[]{:S(2)}, u32[]{:S(2)}) collective-permute-start(f32[2,1,7,1024]{3,2,1,0:T(8,128)S(1)} %get-tuple-element.79), channel_id=1, source_target_pairs={{0,4},{4,8},{8,12},{12,16},{16,20},{20,24},{24,28},{28,0},{1,5},{5... | collective-permute-start | bytes 172040 | tf_op jit(solution)/shard_map/ppermute | solution.py:22
  5.0 10.3 %collective-permute-start.5 = (f32[2,1,7,1024]{3,2,1,0:T(8,128)S(1)}, f32[2,1,7,1024]{3,2,1,0:T(8,128)S(1)}, u32[]{:S(2)}, u32[]{:S(2)}) collective-permute-start(f32[2,1,7,1024]{3,2,1,0:T(8,128)S(1)} %get-tuple-element.80), channel_id=1, source_target_pairs={{4,0},{8,4},{12,8},{16,12},{20,16},{24,20},{28,24},{0,28},{5,1},{9... | collective-permute-start | bytes 172040 | tf_op jit(solution)/shard_map/ppermute | solution.py:25
  9.6 6.2 %collective-permute-start = (f32[3,7,1024]{2,1,0:T(8,128)S(1)}, f32[3,7,1024]{2,1,0:T(8,128)S(1)}, u32[]{:S(2)}, u32[]{:S(2)}) collective-permute-start(f32[3,7,1024]{2,1,0:T(8,128)S(1)} %get-tuple-element.51), channel_id=1, source_target_pairs={{0,4},{4,8},{8,12},{12,16},{16,20},{20,24},{24,28},{28,0},{1,5},{5... | collective-permute-start | bytes 258056 | tf_op jit(solution)/shard_map/ppermute | solution.py:22
  9.7 6.1 %collective-permute-start.1 = (f32[3,7,1024]{2,1,0:T(8,128)S(1)}, f32[3,7,1024]{2,1,0:T(8,128)S(1)}, u32[]{:S(2)}, u32[]{:S(2)}) collective-permute-start(f32[3,7,1024]{2,1,0:T(8,128)S(1)} %get-tuple-element.52), channel_id=1, source_target_pairs={{4,0},{8,4},{12,8},{16,12},{20,16},{24,20},{28,24},{0,28},{5,1},{9... | collective-permute-start | bytes 258056 | tf_op jit(solution)/shard_map/ppermute | solution.py:25
  16.0 11.6 %collective-permute-start.3 = (f32[3,46,7]{2,1,0:T(8,128)S(1)}, f32[3,46,7]{2,1,0:T(8,128)S(1)}, u32[]{:S(2)}, u32[]{:S(2)}) collective-permute-start(f32[3,46,7]{2,1,0:T(8,128)S(1)} %get-tuple-element.39), channel_id=1, source_target_pairs={{1,0},{2,1},{3,2},{0,3},{5,4},{6,5},{7,6},{4,7},{9,8},{10,9},{11,1... | collective-permute-start | bytes 11600 | tf_op jit(solution)/shard_map/ppermute | solution.py:25
  19.3 8.2 %collective-permute-start.2 = (f32[3,46,7]{2,1,0:T(8,128)S(1)}, f32[3,46,7]{2,1,0:T(8,128)S(1)}, u32[]{:S(2)}, u32[]{:S(2)}) collective-permute-start(f32[3,46,7]{2,1,0:T(8,128)S(1)} %get-tuple-element.40), channel_id=1, source_target_pairs={{0,1},{1,2},{2,3},{3,0},{4,5},{5,6},{6,7},{7,4},{8,9},{9,10},{10,1... | collective-permute-start | bytes 11600 | tf_op jit(solution)/shard_map/ppermute | solution.py:22
  19.4 4.7 %collective-permute-start.7 = (f32[2,1,46,7]{3,2,1,0:T(8,128)S(1)}, f32[2,1,46,7]{3,2,1,0:T(8,128)S(1)}, u32[]{:S(2)}, u32[]{:S(2)}) collective-permute-start(f32[2,1,46,7]{3,2,1,0:T(8,128)S(1)} %get-tuple-element.53), channel_id=1, source_target_pairs={{1,0},{2,1},{3,2},{0,3},{5,4},{6,5},{7,6},{4,7},{9,8},{10,9},{11,1... | collective-permute-start | bytes 7736 | tf_op jit(solution)/shard_map/ppermute | solution.py:25
  22.4 5.0 %collective-permute-start.6 = (f32[2,1,46,7]{3,2,1,0:T(8,128)S(1)}, f32[2,1,46,7]{3,2,1,0:T(8,128)S(1)}, u32[]{:S(2)}, u32[]{:S(2)}) collective-permute-start(f32[2,1,46,7]{3,2,1,0:T(8,128)S(1)} %get-tuple-element.54), channel_id=1, source_target_pairs={{0,1},{1,2},{2,3},{3,0},{4,5},{5,6},{6,7},{7,4},{8,9},{9,10},{10,1... | collective-permute-start | bytes 7736 | tf_op jit(solution)/shard_map/ppermute | solution.py:22
  33.3 4.3 %copy-start.2 = (f32[34,1026]{1,0:T(8,128)}, f32[34,1026]{1,0:T(8,128)S(1)}, u32[]{:S(2)}) copy-start(f32[34,1026]{1,0:T(8,128)S(1)} %slice.944) | copy-start | bytes 418612
  33.4 2.3 %copy-start.6 = (f32[38,1030]{1,0:T(8,128)}, f32[38,1030]{1,0:T(8,128)S(1)}, u32[]{:S(2)}) copy-start(f32[38,1030]{1,0:T(8,128)S(1)} %slice.914) | copy-start | bytes 469684
  33.6 3.0 %copy-start.4 = (f32[36,1028]{1,0:T(8,128)}, f32[36,1028]{1,0:T(8,128)S(1)}, u32[]{:S(2)}) copy-start(f32[36,1028]{1,0:T(8,128)S(1)} %slice.928) | copy-start | bytes 444100
  35.4 1.2 copy-start.18
  35.4 1.1 copy-start.20
  35.4 1.1 copy-start.22
  35.4 1.1 copy-start.24
  38.7 1.2 copy-start.42
  38.7 1.1 copy-start.44
  38.7 1.1 copy-start.46
  38.7 1.1 copy-start.48
  79.2 5.5 %collective-permute-start.8 = (f32[2,1,7,1024]{3,2,1,0:T(8,128)S(1)}, f32[2,1,7,1024]{3,2,1,0:T(8,128)S(1)}, u32[]{:S(2)}, u32[]{:S(2)}) collective-permute-start(f32[2,1,7,1024]{3,2,1,0:T(8,128)S(1)} %get-tuple-element.75), channel_id=1, source_target_pairs={{0,4},{4,8},{8,12},{12,16},{16,20},{20,24},{24,28},{28,0},{1,5},{5... | collective-permute-start | bytes 172040 | tf_op jit(solution)/shard_map/ppermute | solution.py:22
  79.3 5.5 %collective-permute-start.9 = (f32[2,1,7,1024]{3,2,1,0:T(8,128)S(1)}, f32[2,1,7,1024]{3,2,1,0:T(8,128)S(1)}, u32[]{:S(2)}, u32[]{:S(2)}) collective-permute-start(f32[2,1,7,1024]{3,2,1,0:T(8,128)S(1)} %get-tuple-element.76), channel_id=1, source_target_pairs={{4,0},{8,4},{12,8},{16,12},{20,16},{24,20},{28,24},{0,28},{5,1},{9... | collective-permute-start | bytes 172040 | tf_op jit(solution)/shard_map/ppermute | solution.py:25
  84.9 8.4 %collective-permute-start.11 = (f32[2,1,46,7]{3,2,1,0:T(8,128)S(1)}, f32[2,1,46,7]{3,2,1,0:T(8,128)S(1)}, u32[]{:S(2)}, u32[]{:S(2)}) collective-permute-start(f32[2,1,46,7]{3,2,1,0:T(8,128)S(1)} %get-tuple-element.49), channel_id=1, source_target_pairs={{1,0},{2,1},{3,2},{0,3},{5,4},{6,5},{7,6},{4,7},{9,8},{10,9},{11,1... | collective-permute-start | bytes 7736 | tf_op jit(solution)/shard_map/ppermute | solution.py:25
  87.4 6.5 %collective-permute-start.10 = (f32[2,1,46,7]{3,2,1,0:T(8,128)S(1)}, f32[2,1,46,7]{3,2,1,0:T(8,128)}, u32[]{:S(2)}, u32[]{:S(2)}) collective-permute-start(f32[2,1,46,7]{3,2,1,0:T(8,128)S(1)} %get-tuple-element.50), channel_id=1, source_target_pairs={{0,1},{1,2},{2,3},{3,0},{4,5},{5,6},{6,7},{7,4},{8,9},{9,10},{10,1... | collective-permute-start | bytes 7736 | tf_op jit(solution)/shard_map/ppermute | solution.py:22
  95.0 1.4 copy-start.1
  96.3 1.5 copy-start.9
  96.3 1.5 copy-start.11
  96.3 1.5 copy-start.13
  96.3 1.5 copy-start.15
  96.4 1.5 copy-start.17
  97.8 1.4 copy-start.7
  97.8 1.4 copy-start.35
  97.8 1.4 copy-start.37
  97.9 1.4 copy-start.39
  97.9 1.4 copy-start.41
  99.2 1.4 copy-start.5
  99.2 1.4 copy-start.19
  99.2 1.4 copy-start.21
  99.3 1.4 copy-start.23
  99.3 1.4 copy-start.25
  101.2 1.1 copy-start.29
  101.3 1.2 copy-start.31
  101.3 1.2 copy-start.33
  102.5 1.0 copy-start.47
  102.5 1.1 copy-start.49
  (19 other events, 16.0 us)
where the time goes:
time: 154 us
  blocking collectives  77.4 us (50%)
  other arithmetic  23.4 us (15%)
  local copies, waits for them, and re-layouts  21.2 us (14%)
  starting transfers between devices  20.6 us (13%)
  waiting for transfers between devices  6.73 us (4%)
  between operations  4.29 us (3%)
    psum x2, blocking collectives, per_device(): term_total, state_total = lax.psum((term_local, state_local), ('gx', 'gy'))  77.4 us
    ppermute x6, starting transfers between devices, padded(): lax.ppermute(lax.slice_in_dim(block, 0, width, axis=dim), axis, backward)  19.9 us
    another operation x2, local copies, waits for them, and re-layouts, per_device(): jnp.stack([jnp.sum(vector * vector, axis=(0, 2, 3)) for vector in chebysh...  10.4 us
    reduce_sum x12, other arithmetic, per_device(): jnp.sum(vector * vector, axis=(0, 2, 3))  9.75 us
    sub x10, other arithmetic, per_device(): following = 2.0 * applied - shrink(previous, previous_margin - margin + 1)  5.76 us
    ppermute x6, waiting for transfers between devices, padded(): lax.ppermute(lax.slice_in_dim(block, block.shape[dim] - width, None, axis...  4.9 us
    unnamed x110, local copies, waits for them, and re-layouts  3.2 us
  transfers between devices with their start and end apart: 12, of which 4 were waited for; matrix products, arithmetic and copies ran while one was open for 5% of the time, Pallas kernels for 0%

commit v1 on v0

v1 whole, which is shorter than its diff:
```python
import functools
import math

import jax
import jax.numpy as jnp
from jax import lax
from jax.experimental import pallas as pl
from jax.experimental.pallas import tpu as pltpu
from jax.sharding import PartitionSpec as P

TERMS = 8
STEPS = 2
SPECTRAL = 7.5
EPSILON = 1e-06
REACH = TERMS - 1
DEPTH = STEPS * REACH
SUB = 8
LANES = 128
SLOT = 16
HALO = -(-DEPTH // SUB) * SUB
PAD = SUB
MESH = pl.DeviceIdType.MESH


def signed(degree):
    return (((0, 1), (1, 1)), ((1, 1), (0, -1)), ((0, -1), (1, -1)), ((1, -1), (0, 1)))[degree % 4]


def bessel_weights(duration):
    halved = duration * (SPECTRAL * 0.5)
    square = halved * halved
    weights = []
    power = jnp.ones_like(halved)
    for degree in range(TERMS):
        series = power * (1.0 / math.factorial(degree))
        summed = series
        for counter in range(1, 24):
            series = series * (square * (-1.0 / (counter * (counter + degree))))
            summed = summed + series
        weights.append(summed if degree == 0 else 2.0 * summed)
        power = power * halved
    return weights


def falloff(position, centre, extent):
    position = jnp.where(position < 0, position + extent, position)
    position = jnp.where(position >= extent, position - extent, position)
    distance = position - centre
    distance = jnp.where(distance < 0, distance + extent, distance)
    distance = jnp.minimum(distance, extent - distance).astype(jnp.float32)
    return jnp.exp(-(distance * distance * (4.5 / (extent * extent))))


def kernel(
    gx, gy, table_ref, centre_ref, duration_ref, re_hbm, im_hbm, on_hbm, bx_hbm, by_hbm,
    out_re, out_im, scale_ref, norms_ref,
    in_re, in_im, in_on, in_bx, in_by, main, odd, first, pack, edge, message, slots,
    load_sem, send_sem, recv_sem, sum_send, sum_recv,
):
    rows, cols = in_on.shape
    tiles = cols // LANES
    extended = rows + 2 * HALO
    me_x, me_y = lax.axis_index("gx"), lax.axis_index("gy")
    devices = gx * gy
    me = me_x * gy + me_y

    barrier = pltpu.get_barrier_semaphore()

    def peer(step):
        other = lax.rem(me + step, devices)
        return (other // gy, lax.rem(other, gy))

    def greet(step, carry):
        pl.semaphore_signal(barrier, inc=1, device_id=peer(step), device_id_type=MESH)
        return carry

    loads = [
        pltpu.make_async_copy(source, target, load_sem.at[index])
        for index, (source, target) in enumerate(
            ((by_hbm, in_by), (bx_hbm, in_bx), (on_hbm, in_on), (re_hbm.at[0], in_re), (im_hbm.at[0], in_im))
        )
    ]
    for load in loads:
        load.start()
    lax.fori_loop(1, devices, greet, 0)

    lane = lax.broadcasted_iota(jnp.int32, (SUB, LANES), 1)
    sublane = lax.broadcasted_iota(jnp.int32, (SUB, LANES), 0)
    table = jnp.zeros((SUB, LANES), jnp.float32)
    for index in range(table_ref.shape[0]):
        table = jnp.where(lane == index, table_ref[index], table)
    table = table * (2.0 / SPECTRAL)
    weights = bessel_weights(jnp.full((SUB, LANES), duration_ref[0], jnp.float32))
    row_env = [
        falloff(me_x * rows + tile * SUB + sublane, centre_ref[0, 0], gx * rows)
        for tile in range(rows // SUB)
    ]
    col_env = [
        falloff(me_y * cols + tile * LANES + lane, centre_ref[0, 1], gy * cols)
        for tile in range(tiles)
    ]
    for load in loads:
        load.wait()

    def lookup(index):
        return jnp.take_along_axis(table, index, axis=1, mode="promise_in_bounds")

    own = PAD + HALO
    start_norm = jnp.zeros((SUB, LANES), jnp.float32)
    for r in range(rows // SUB):
        span = slice(r * SUB, r * SUB + SUB)
        held = slice(own + r * SUB, own + r * SUB + SUB)
        for t in (0, tiles - 1, *range(1, tiles - 1)):
            across = slice(t * LANES, t * LANES + LANES)
            envelope = row_env[r] * col_env[t]
            values = (
                in_re[span, across] * envelope,
                in_im[span, across] * envelope,
                in_on[span, across] * (2.0 / SPECTRAL),
                lookup(in_bx[span, across]),
                lookup(in_by[span, across]),
            )
            start_norm = start_norm + (values[0] * values[0] + values[1] * values[1])
            for a, value in enumerate(values):
                main[a, t, held, :] = value
            if t == 0:
                packed = values[0]
                for a in range(1, 5):
                    moved = pltpu.roll(values[a], SLOT * a, 1)
                    packed = jnp.where(lane >= SLOT * a, moved, packed)
                pack[0, span, :] = packed
            if t == tiles - 1:
                packed = pltpu.roll(values[0], SLOT, 1)
                for a in range(1, 5):
                    moved = pltpu.roll(values[a], SLOT * (a + 1), 1)
                    packed = jnp.where(lane >= SLOT * a, moved, packed)
                pack[1, span, :] = packed

    pl.semaphore_wait(barrier, devices - 1)
    up, down = lax.rem(me_x + gx - 1, gx), lax.rem(me_x + 1, gx)
    west, east = lax.rem(me_y + gy - 1, gy), lax.rem(me_y + 1, gy)
    top, bottom = pl.ds(0, HALO), pl.ds(rows - HALO, HALO)
    copies = []

    def send(source, target, device):
        index = len(copies)
        copy = pltpu.make_async_remote_copy(
            src_ref=source, dst_ref=target, send_sem=send_sem.at[index], recv_sem=recv_sem.at[index],
            device_id=device, device_id_type=MESH,
        )
        copy.start()
        copies.append(copy)

    body = pl.ds(0, tiles)
    for side, aside in ((0, west), (1, east)):
        send(pack.at[side], edge.at[side, pl.ds(HALO, rows)], (me_x, aside))
        send(pack.at[side, top], edge.at[side, pl.ds(HALO + rows, HALO)], (up, aside))
        send(pack.at[side, bottom], edge.at[side, pl.ds(0, HALO)], (down, aside))
    send(
        main.at[:, body, pl.ds(own, HALO)],
        main.at[:, body, pl.ds(own + rows, HALO)],
        (up, me_y),
    )
    send(
        main.at[:, body, pl.ds(own + rows - HALO, HALO)],
        main.at[:, body, pl.ds(PAD, HALO)],
        (down, me_y),
    )
    for copy in copies[:6]:
        copy.wait()
    for r in range(extended // SUB):
        span = slice(r * SUB, r * SUB + SUB)
        held = slice(PAD + r * SUB, PAD + r * SUB + SUB)
        from_east = edge[0, span, :]
        from_west = edge[1, span, :]
        for a in range(5):
            right = pltpu.roll(from_east, (LANES - SLOT * a) % LANES, 1)
            left = pltpu.roll(from_west, (LANES - SLOT * (a + 1)) % LANES, 1)
            main[a, tiles, held, :] = jnp.where(lane < LANES // 2, right, left)
    for copy in copies[6:]:
        copy.wait()

    last_lane = lane == LANES - 1
    first_lane = lane == 0

    def apply(current, target, degree, left_over, total, is_last):
        low = (HALO - left_over) // SUB
        high = -(-(HALO + rows + left_over) // SUB)
        keep = (HALO // SUB, (HALO + rows) // SUB)
        later = left_over if is_last else left_over + degree - REACH
        norm = jnp.zeros((SUB, LANES), jnp.float32)
        for r in range(low, high):
            base = PAD + r * SUB
            here = slice(base, base + SUB)
            above = slice(base - 1, base + SUB - 1)
            below = slice(base + 1, base + SUB + 1)
            owned = keep[0] <= r < keep[1]
            centre = [[current[f, t, here, :] for f in range(2)] for t in range(tiles + 1)]
            cross = [main[4, t, here, :] for t in range(tiles + 1)]
            rights = [[pltpu.roll(centre[t][f], LANES - 1, 1) for f in range(2)] for t in range(tiles + 1)]
            lefts = [[pltpu.roll(cross[t] * centre[t][f], 1, 1) for f in range(2)] for t in range(tiles + 1)]
            for t in range(tiles + 1):
                potential = main[2, t, here, :]
                hop_below = main[3, t, here, :]
                hop_above = main[3, t, above, :]
                fresh = []
                for f in range(2):
                    right = jnp.where(last_lane, rights[(t + 1) % (tiles + 1)][f], rights[t][f])
                    left = jnp.where(first_lane, lefts[t - 1][f], lefts[t][f])
                    value = potential * centre[t][f]
                    value = value - hop_below * current[f, t, below, :]
                    value = value - hop_above * current[f, t, above, :]
                    value = value - cross[t] * right
                    value = value - left
                    if degree == 1:
                        value = value * 0.5
                    else:
                        value = value - target[f, t, here, :]
                    target[f, t, here, :] = value
                    fresh.append(value)
                mine = owned and t < tiles
                if mine:
                    norm = norm + (fresh[0] * fresh[0] + fresh[1] * fresh[1])
                total(r, t, degree, centre[t], fresh, mine)
        return norm

    norms = []
    sums = []

    reach_tiles = ((HALO - REACH) // SUB, -(-(HALO + rows + REACH) // SUB))
    state = {}

    def accumulate(read, write, step):
        def total(r, t, degree, before, fresh, mine):
            if step == STEPS - 1:
                if not mine:
                    return
            elif not reach_tiles[0] <= r < reach_tiles[1]:
                return
            result = []
            for part, (f, sign) in enumerate(signed(degree)):
                base = weights[0] * before[part] if degree == 1 else read(part, r, t)
                term = weights[degree] * fresh[f]
                result.append(base + term if sign > 0 else base - term)
            for part in range(2):
                write(part, r, t, result[part])
            if degree == REACH and mine:
                state["sum"] = state["sum"] + (result[0] * result[0] + result[1] * result[1])
        return total

    def read_first(part, r, t):
        return first[part, t, PAD + r * SUB : PAD + r * SUB + SUB, :]

    def write_first(part, r, t, value):
        first[part, t, PAD + r * SUB : PAD + r * SUB + SUB, :] = value

    outs = (out_re, out_im)

    def place(r, t):
        begin = r * SUB - HALO
        return (0, slice(begin, begin + SUB), slice(t * LANES, t * LANES + LANES))

    def read_out(part, r, t):
        return outs[part][place(r, t)]

    def write_out(part, r, t, value):
        outs[part][place(r, t)] = value

    psi = main
    norms.append(start_norm)
    for step in range(STEPS):
        total = accumulate(*((read_first, write_first) if step == 0 else (read_out, write_out)), step)
        state["sum"] = jnp.zeros((SUB, LANES), jnp.float32)
        if step:
            norms.append(sums[-1])
        buffers = (psi, odd)
        for degree in range(1, TERMS):
            left_over = DEPTH - step * REACH - degree
            norms.append(apply(buffers[(degree + 1) % 2], buffers[degree % 2], degree, left_over, total, step == STEPS - 1))
        sums.append(state["sum"])
        psi = first

    entries = norms + sums
    row = jnp.zeros((1, LANES), jnp.float32)
    for begin in range(0, len(entries), SUB):
        grid = jnp.zeros((SUB, LANES), jnp.float32)
        for offset, entry in enumerate(entries[begin : begin + SUB]):
            grid = jnp.where(sublane == offset, jnp.sum(entry, axis=0, keepdims=True), grid)
        grid = jnp.sum(grid, axis=1, keepdims=True)
        row = row + jnp.sum(jnp.where(lane == sublane + begin, grid, 0.0), axis=0, keepdims=True)
    message[...] = row

    def copy_of(step):
        return pltpu.make_async_remote_copy(
            src_ref=message, dst_ref=slots.at[me], send_sem=sum_send, recv_sem=sum_recv,
            device_id=peer(step), device_id_type=MESH,
        )

    slots[me] = row

    def send_sum(step, carry):
        copy_of(step).start()
        return carry

    lax.fori_loop(1, devices, send_sum, 0)
    others = slots.at[pl.ds(0, devices - 1)]
    pltpu.make_async_copy(others, others, sum_send).wait()
    pltpu.make_async_copy(others, others, sum_recv).wait()
    whole = jnp.sum(slots[...], axis=0) * (1.0 / (devices * rows * cols))
    lane_row = lax.broadcasted_iota(jnp.int32, (1, LANES), 1)
    count = STEPS * TERMS

    def entry_of(index):
        return jnp.sum(jnp.where(lane_row == index, whole, 0.0), axis=1, keepdims=True)

    scale = jnp.ones((1, 1), jnp.float32)
    factor = jnp.ones((1, LANES), jnp.float32)
    for step in range(STEPS):
        factor = jnp.where((lane_row >= step * TERMS) & (lane_row < (step + 1) * TERMS), scale * scale, factor)
        scale = scale * lax.rsqrt(entry_of(count + step) * (scale * scale) + EPSILON)
    norms_ref[...] = whole * factor
    scale_ref[...] = jnp.broadcast_to(scale, (1, LANES))


def per_device(gx, gy, init_re, init_im, onsite, bond_x, bond_y, hop_table, centre, duration):
    packets, rows, cols = init_re.shape
    tiles = cols // LANES
    assert packets == 1 and rows >= HALO
    height = rows + 2 * HALO + 2 * PAD
    f32, i32 = jnp.float32, jnp.int32
    smem = pl.BlockSpec(memory_space=pltpu.SMEM)
    vmem = pl.BlockSpec(memory_space=pltpu.VMEM)
    anywhere = pl.BlockSpec(memory_space=pl.ANY)
    raw_re, raw_im, scale, norms = pl.pallas_call(
        functools.partial(kernel, gx, gy),
        out_shape=(
            jax.ShapeDtypeStruct(init_re.shape, f32),
            jax.ShapeDtypeStruct(init_im.shape, f32),
            jax.ShapeDtypeStruct((1, LANES), f32),
            jax.ShapeDtypeStruct((1, LANES), f32),
        ),
        in_specs=[smem] * 3 + [anywhere] * 5,
        out_specs=[vmem] * 4,
        scratch_shapes=[
            pltpu.VMEM((rows, cols), f32),
            pltpu.VMEM((rows, cols), f32),
            pltpu.VMEM((rows, cols), f32),
            pltpu.VMEM((rows, cols), i32),
            pltpu.VMEM((rows, cols), i32),
            pltpu.VMEM((5, tiles + 1, height, LANES), f32),
            pltpu.VMEM((2, tiles + 1, height, LANES), f32),
            pltpu.VMEM((2, tiles + 1, height, LANES), f32),
            pltpu.VMEM((2, rows, LANES), f32),
            pltpu.VMEM((2, rows + 2 * HALO, LANES), f32),
            pltpu.VMEM((1, LANES), f32),
            pltpu.VMEM((gx * gy, 1, LANES), f32),
            pltpu.SemaphoreType.DMA((5,)),
            pltpu.SemaphoreType.DMA((8,)),
            pltpu.SemaphoreType.DMA((8,)),
            pltpu.SemaphoreType.DMA,
            pltpu.SemaphoreType.DMA,
        ],
        compiler_params=pltpu.CompilerParams(collective_id=0, has_side_effects=True),
        name="chebyshev",
    )(hop_table, centre, duration, init_re, init_im, onsite, bond_x, bond_y)
    factor = scale[0, 0]
    table = norms[0, : STEPS * TERMS].reshape(STEPS, TERMS, 1)
    return raw_re * factor, raw_im * factor, table


def solution(mesh):
    return jax.shard_map(
        functools.partial(per_device, mesh.shape["gx"], mesh.shape["gy"]),
        mesh=mesh,
        in_specs=(
            P(None, "gx", "gy"),
            P(None, "gx", "gy"),
            P("gx", "gy"),
            P("gx", "gy"),
            P("gx", "gy"),
            P(),
            P(),
            P(),
        ),
        out_specs=(P(None, "gx", "gy"), P(None, "gx", "gy"), P()),
        check_vma=False,
    )
```

time: 154 us -> 31.4 us (0.20)
  blocking collectives: 77.4 us -> 0 us
  Pallas kernels: 0 us -> 26.3 us
  other arithmetic: 23.4 us -> 1.72 us
  starting transfers between devices: 20.6 us -> 0 us
  local copies, waits for them, and re-layouts: 21.2 us -> 1.91 us
  waiting for transfers between devices: 6.73 us -> 0 us
  between operations: 4.29 us -> 1.3 us
    psum x2 -> x0, blocking collectives: 77.4 us -> none  [per_device(): term_total, state_total = lax.psum((term_local, state_local), ('gx', 'gy'))]
    pallas_call x0 -> x1, Pallas kernels: none -> 26.3 us  [per_device(): pl.pallas_call(functools.partial(kernel, gx, gy), out_shape=(jax.ShapeDty...]
    ppermute x12 -> x0, starting transfers between devices: 20.6 us -> none  [the longest x6 19.9 us: padded(): lax.ppermute(lax.slice_in_dim(block, 0, width, axis=dim), axis, backward)]
    reduce_sum x15 -> x0, other arithmetic: 12 us -> none  [the longest x12 9.75 us: per_device(): jnp.sum(vector * vector, axis=(0, 2, 3))]
    another operation x2 -> x1, local copies, waits for them, and re-layouts: 10.4 us -> 0.64 us  [per_device(): table = norms[0, :STEPS * TERMS].reshape(STEPS, TERMS, 1)]
    ppermute x12 -> x0, waiting for transfers between devices: 6.73 us -> none  [the longest x6 4.9 us: padded(): lax.ppermute(lax.slice_in_dim(block, block.shape[dim] - width, None, axis...]
    sub x10 -> x0, other arithmetic: 5.76 us -> none  [per_device(): following = 2.0 * applied - shrink(previous, previous_margin - margin + 1)]
    slice x19 -> x1, local copies, waits for them, and re-layouts: 3.86 us -> 0.02 us  [per_device(): table = norms[0, :STEPS * TERMS].reshape(STEPS, TERMS, 1)]
  transfers between devices with their start and end apart: 12 -> 0, of which waited for: 4 -> 0; matrix products, arithmetic and copies ran while one was open for 5% -> 0% of each run, Pallas kernels for 0% -> 0%
where the time goes in v1:
time: 31.4 us; the launch traced here: 31.2 us
  Pallas kernels  26.3 us (84%)
  local copies, waits for them, and re-layouts  1.91 us (6%)
  other arithmetic  1.72 us (5%)
  between operations  1.3 us (4%)
    pallas_call x1, Pallas kernels, per_device(): pl.pallas_call(functools.partial(kernel, gx, gy), out_shape=(jax.ShapeDty...  26.3 us
    mul x1, other arithmetic, per_device(): return (raw_re * factor, raw_im * factor, table)  1.72 us
    unnamed x4, local copies, waits for them, and re-layouts  1.24 us
    another operation x1, local copies, waits for them, and re-layouts, per_device(): table = norms[0, :STEPS * TERMS].reshape(STEPS, TERMS, 1)  0.64 us

profile of v1, /device:TPU:0, one launch (start us, length us, event | category | flops | bytes accessed | tf_op | source)
XLA Modules:
  0.0 31.2 jit_solution(10582612983208796806)
XLA Ops:
  1.3 26.3 %chebyshev.1 = (f32[1,32,1024]{2,1,0:T(8,128)}, f32[1,32,1024]{2,1,0:T(8,128)}, f32[1,128]{1,0:T(1,128)}, f32[1,128]{1,0:T(1,128)}) custom-call(f32[16]{0:T(128)} %table_ref.1, s32[1,2]{1,0:T(1,128)} %centre_ref.1, f32[1]{0:T(128)S(6)} %copy.12.duration_ref, f32[1,32,1024]{2,1,0:T(8,128)} %re_hbm.1, f32[1,32,1024]{2,1,0:T(8,128)} %im_hbm.1, ...), custom_call_target="tpu_custom_call" | custom-call | tf_op jit(solution)/shard_map/chebyshev/pallas_call | solution.py:334
  27.6 0.0 copy-start
  27.6 0.6 %copy-done = f32[1,128]{1,0:T(1,128)S(1)} copy-done((f32[1,128]{1,0:T(1,128)S(1)}, f32[1,128]{1,0:T(1,128)}, u32[]{:S(2)}) %copy-start) | copy-done | bytes 536
  28.2 1.7 %broadcast_multiply_fusion = (f32[1,32,1024]{2,1,0:T(8,128)}, f32[1,32,1024]{2,1,0:T(8,128)}) fusion(f32[1,32,1024]{2,1,0:T(8,128)} %get-tuple-element.9, f32[]{:T(128)S(1)} %bitcast.3, f32[1,32,1024]{2,1,0:T(8,128)} %get-tuple-element.7), kind=kLoop, calls=%fused_computation | loop fusion | flops 65536 | bytes 524292 | tf_op jit(solution)/shard_map/mul | solution.py:368
  29.9 0.0 copy-start.1
  29.9 0.7 %copy-done.1 = f32[1,128]{1,0:T(1,128)S(1)} copy-done((f32[1,128]{1,0:T(1,128)S(1)}, f32[1,128]{1,0:T(1,128)}, u32[]{:S(2)}) %copy-start.1) | copy-done | bytes 536
  30.6 0.6 %reshape_squeeze.3 = f32[2,8,1]{1,0,2:T(2,128)} reshape(f32[16]{0:T(128)S(1)} %slice_reduce_fusion) | data formatting | bytes 128 | tf_op jit(solution)/shard_map/reshape;squeeze | solution.py:367
  (1 shorter events, 0.0 us)
Async XLA Ops:
  27.6 0.6 %copy-start = (f32[1,128]{1,0:T(1,128)S(1)}, f32[1,128]{1,0:T(1,128)}, u32[]{:S(2)}) copy-start(f32[1,128]{1,0:T(1,128)} %get-tuple-element.8) | copy-start | bytes 1540
  29.9 0.7 %copy-start.1 = (f32[1,128]{1,0:T(1,128)S(1)}, f32[1,128]{1,0:T(1,128)}, u32[]{:S(2)}) copy-start(f32[1,128]{1,0:T(1,128)} %get-tuple-element.10) | copy-start | bytes 1540
